TPU v7x, 32 devices: a whole 2x2x4 slice. The times are simulated.
32 devices in a mesh: seq: 4 (over y, x), fsdp: 8 (over z, core).
Axes of the slice: x: 2, y: 2, z: 4, core: 2. Of those that a mesh axis runs over, the one named last changes fastest.
Arguments:
- tokens: bfloat16 [8, 1024, 1536], P('fsdp', 'seq'), may hold values from -6 to 6
- mixing_weight: bfloat16 [1536, 2560], P(('seq', 'fsdp')), may hold values from -0.21875 to 0.21875
- output_weight: bfloat16 [1536, 1536], P(('seq', 'fsdp')), may hold values from -0.625 to 0.625
- norm_gains: bfloat16 [1536, 2], P(('seq', 'fsdp')), may hold values from 0.099609375 to 1.8984375
- expert_gate: bfloat16 [1536, 40, 512], P('fsdp', 'seq'), may hold values from -0.15625 to 0.15625
- expert_up: bfloat16 [1536, 40, 512], P('fsdp', 'seq'), may hold values from -0.15625 to 0.15625
- expert_down: bfloat16 [1536, 40, 512], P('fsdp', 'seq'), may hold values from -1.25 to 1.25
- gate_logits: float32 [8, 1024, 8], P('fsdp'), may hold values from -3 to 3
- routes: int32 [8, 1024, 8], P('fsdp'), may hold values from 0 to 39, all different within a row
- fill_order: int32 [8, 1024], P('fsdp'), may hold values from 0 to 1023, each once within a row
- cotangent: bfloat16 [8, 1024, 1536], P('fsdp', 'seq'), may hold values from -6 to 6
Outputs:
- layer_output: bfloat16 [8, 1024, 1536], P('fsdp', 'seq')
- tokens_gradient: float32 [8, 1024, 1536], P('fsdp', 'seq')
- mixing_gradient: float32 [1536, 2560], P(('seq', 'fsdp'))
- output_gradient: float32 [1536, 1536], P(('seq', 'fsdp'))
- gains_gradient: float32 [1536, 2], P(('seq', 'fsdp'))
- gate_gradient: float32 [1536, 40, 512], P('fsdp', 'seq')
- up_gradient: float32 [1536, 40, 512], P('fsdp', 'seq')
- down_gradient: float32 [1536, 40, 512], P('fsdp', 'seq')
- logits_gradient: float32 [8, 1024, 8], P('fsdp', 'seq')
Inputs may be any that keep to these rules, and one draw needn't show every extreme that they name: `routes`: each token names 8 different experts. `fill_order`: each sequence's row holds each token index of that sequence once.
All inputs are finite; a program needn't handle non-finite values.
Results may differ from a plain program's by a relative error of at most 0.017.
The roundings to bfloat16 on the way count: a program that leaves them out, or rounds other values in their place, can miss the bound.
Values may be sent and summed in bfloat16 or wider, within the bound.
A program may use at most 256 MiB of HBM per device.

v0:
```python
import math
import jax
import jax.numpy as jnp
from jax import lax
from jax.sharding import PartitionSpec as P

D = 1536
HEADS = 24
KV_HEADS = 8
HEAD_DIM = 64
FF = 512
EXPERTS = 40
TOP = 8
QBLK = 512
epsilon = 1e-05
rope_base = 10000.0


def norm_apply(values, gain_row):
    return (
        values * lax.rsqrt(jnp.mean(values * values, axis=-1, keepdims=True) + epsilon) * gain_row
    )


def rotary_tables(positions):
    half_width = HEAD_DIM // 2
    frequency = rope_base ** (-2.0 * jnp.arange(half_width, dtype=jnp.float32) / HEAD_DIM)
    angles = positions.astype(jnp.float32)[:, None] * frequency[None, :]
    cos_table = jnp.cos(angles)
    sin_table = jnp.sin(angles)
    return (jnp.concatenate([cos_table, cos_table], 1), jnp.concatenate([sin_table, sin_table], 1))


def rotate(values, cos_table, sin_table):
    half_width = values.shape[-1] // 2
    turned = jnp.concatenate([-values[..., half_width:], values[..., :half_width]], -1)
    return values * cos_table[:, None, :] + turned * sin_table[:, None, :]


def softmax_last(logit_rows):
    row_max = jnp.max(logit_rows, axis=-1, keepdims=True)
    exponent = jnp.exp(logit_rows - row_max)
    return exponent / jnp.sum(exponent, axis=-1, keepdims=True)


def build_slots(route_rows, order_rows, expert_ids, capacity):
    length = route_rows.shape[0]
    chosen = route_rows[:, :, None] == expert_ids[None, None, :]
    hit_count = jnp.sum(chosen.astype(jnp.int32), axis=1)
    ordered = hit_count[order_rows]
    before = jnp.cumsum(ordered, axis=0) - ordered
    slot_rank = jnp.zeros_like(before).at[order_rows].set(before)
    kept_mask = (hit_count > 0) & (slot_rank < capacity)
    slot_place = jnp.where(kept_mask, slot_rank, capacity)
    expert_cols = jnp.broadcast_to(
        jnp.arange(expert_ids.shape[0], dtype=jnp.int32)[None, :], slot_place.shape
    )
    token_ids = jnp.broadcast_to(jnp.arange(length, dtype=jnp.int32)[:, None], slot_place.shape)
    table_full = jnp.full((expert_ids.shape[0], capacity + 1), length, jnp.int32)
    table_full = table_full.at[expert_cols, slot_place].set(token_ids)
    return (chosen, table_full[:, :capacity])


def local(
    tokens,
    mixing_weight,
    output_weight,
    norm_gains,
    expert_gate,
    expert_up,
    expert_down,
    gate_logits,
    routes,
    fill_order,
    cotangent,
):
    single = jnp.float32
    narrow = jnp.bfloat16
    groups = lax.axis_size("seq")
    column = lax.axis_index("seq")
    tok_rows = tokens.shape[1]
    seq_len = tok_rows * groups
    capacity = (seq_len * TOP + EXPERTS - 1) // EXPERTS
    local_count = expert_gate.shape[1]
    query_width = HEADS * HEAD_DIM
    key_width = KV_HEADS * HEAD_DIM
    mixing_width = query_width + 2 * key_width
    score_scale = 1.0 / math.sqrt(HEAD_DIM)
    group_size = HEADS // KV_HEADS
    inputs = tokens[0].astype(single)
    mixing_full, exit_full, gains_full = (
        lax.all_gather(mixing_weight, ("seq", "fsdp"), axis=0, tiled=True),
        lax.all_gather(output_weight, ("seq", "fsdp"), axis=0, tiled=True),
        lax.all_gather(norm_gains, ("seq", "fsdp"), axis=0, tiled=True),
    )
    gains_float = gains_full.astype(single)
    normed = norm_apply(inputs, gains_float[:, 0])
    normed_low = normed.astype(narrow)
    projected = jnp.dot(normed_low, mixing_full, preferred_element_type=single)
    positions = column * tok_rows + jnp.arange(tok_rows, dtype=jnp.int32)
    cos_table, sin_table = rotary_tables(positions)
    query_raw = projected[:, :query_width].reshape(tok_rows, HEADS, HEAD_DIM)
    key_raw = projected[:, query_width : query_width + key_width].reshape(
        tok_rows, KV_HEADS, HEAD_DIM
    )
    query_send = (
        rotate(query_raw, cos_table, sin_table).reshape(tok_rows, query_width).astype(narrow)
    )
    key_send = rotate(key_raw, cos_table, sin_table).reshape(tok_rows, key_width).astype(narrow)
    value_send = projected[:, query_width + key_width :].astype(narrow)
    query_heads, key_heads, value_heads = (
        lax.all_to_all(query_send, "seq", split_axis=1, concat_axis=0, tiled=True),
        lax.all_to_all(key_send, "seq", split_axis=1, concat_axis=0, tiled=True),
        lax.all_to_all(value_send, "seq", split_axis=1, concat_axis=0, tiled=True),
    )
    local_kv = key_heads.shape[1] // HEAD_DIM
    blocks = seq_len // QBLK
    query_blocks = query_heads.reshape(blocks, QBLK, local_kv, group_size, HEAD_DIM)
    key_heads = key_heads.reshape(seq_len, local_kv, HEAD_DIM)
    value_heads = value_heads.reshape(seq_len, local_kv, HEAD_DIM)
    starts = jnp.arange(blocks, dtype=jnp.int32) * QBLK
    key_pos = jnp.arange(seq_len, dtype=jnp.int32)

    def block_scores(row_block, first_row):
        scores = (
            jnp.einsum("bkgd,tkd->kgbt", row_block, key_heads, preferred_element_type=single)
            * score_scale
        )
        allowed = (first_row + jnp.arange(QBLK, dtype=jnp.int32))[:, None] >= key_pos[None, :]
        return jnp.where(allowed, scores, -jnp.inf)

    def attend(block_items):
        row_block, first_row = block_items
        scores = block_scores(row_block, first_row)
        row_max = jnp.max(scores, axis=-1, keepdims=True)
        exponent = jnp.exp(scores - row_max)
        row_total = jnp.sum(exponent, axis=-1, keepdims=True)
        soft_weights = (exponent / row_total).astype(narrow)
        attended = jnp.einsum(
            "kgbt,tkd->bkgd", soft_weights, value_heads, preferred_element_type=single
        )
        return (attended.astype(narrow), (row_max + jnp.log(row_total))[..., 0])

    attended_blocks, log_totals = lax.map(attend, (query_blocks, starts))
    attended_heads = attended_blocks.reshape(seq_len, -1)
    attn_rows = lax.all_to_all(attended_heads, "seq", split_axis=0, concat_axis=1, tiled=True)
    attn_out = lax.dot_general(
        attn_rows, exit_full, (((1,), (1,)), ((), ())), preferred_element_type=single
    )
    hidden = inputs + attn_out
    normed_two = norm_apply(hidden, gains_float[:, 1])
    normed_two_low = normed_two.astype(narrow)
    seq_rows = lax.all_gather(normed_two_low, "seq", axis=0, tiled=True)
    expert_ids = column * local_count + jnp.arange(local_count, dtype=jnp.int32)
    gating = softmax_last(gate_logits[0])
    chosen, slot_table = build_slots(routes[0], fill_order[0], expert_ids, capacity)
    chosen_float = chosen.astype(single)
    token_weight = jnp.sum(gating[:, :, None] * chosen_float, axis=1)
    padded_weight = jnp.concatenate([token_weight, jnp.zeros((1, local_count), single)], 0)
    expert_cols = jnp.arange(local_count, dtype=jnp.int32)[:, None]
    slot_weight = padded_weight[slot_table, expert_cols]
    padded_rows = jnp.concatenate([seq_rows, jnp.zeros((1, D), narrow)], 0)
    slot_rows = padded_rows[slot_table]
    gate_full, up_full, down_full = (
        lax.all_gather(expert_gate, "fsdp", axis=0, tiled=True),
        lax.all_gather(expert_up, "fsdp", axis=0, tiled=True),
        lax.all_gather(expert_down, "fsdp", axis=0, tiled=True),
    )
    gate_pre = jnp.einsum("ecd,def->ecf", slot_rows, gate_full, preferred_element_type=single)
    up_pre = jnp.einsum("ecd,def->ecf", slot_rows, up_full, preferred_element_type=single)
    sigmoid_gate = jax.nn.sigmoid(gate_pre)
    mid_low = (gate_pre * sigmoid_gate * up_pre).astype(narrow)
    expert_out = jnp.einsum("ecf,def->ecd", mid_low, down_full, preferred_element_type=single)
    partial_sum = (
        jnp.zeros((seq_len + 1, D), single)
        .at[slot_table]
        .add(expert_out * slot_weight[:, :, None])[:seq_len]
    )
    moe_rows = lax.psum_scatter(
        partial_sum.astype(jnp.bfloat16), "seq", scatter_dimension=0, tiled=True
    ).astype(jnp.float32)
    layer_output = (hidden + moe_rows).astype(narrow)[None]
    cot_rows = lax.all_gather(cotangent[0], "seq", axis=0, tiled=True)
    padded_cot = jnp.concatenate([cot_rows, jnp.zeros((1, D), narrow)], 0)
    slot_cot = padded_cot[slot_table].astype(single)
    slot_weight_grad = jnp.sum(slot_cot * expert_out, axis=-1)
    out_low = (slot_cot * slot_weight[:, :, None]).astype(narrow)
    gate_full, up_full, down_full = (
        lax.all_gather(expert_gate, "fsdp", axis=0, tiled=True),
        lax.all_gather(expert_up, "fsdp", axis=0, tiled=True),
        lax.all_gather(expert_down, "fsdp", axis=0, tiled=True),
    )
    mid_grad = jnp.einsum("ecd,def->ecf", out_low, down_full, preferred_element_type=single)
    gate_grad_low = (
        mid_grad * up_pre * sigmoid_gate * (1.0 + gate_pre * (1.0 - sigmoid_gate))
    ).astype(narrow)
    up_grad_low = (mid_grad * gate_pre * sigmoid_gate).astype(narrow)
    row_grad = jnp.einsum("ecf,def->ecd", gate_grad_low, gate_full, preferred_element_type=single)
    row_grad = row_grad + jnp.einsum(
        "ecf,def->ecd", up_grad_low, up_full, preferred_element_type=single
    )
    normed_two_part = jnp.zeros((seq_len + 1, D), single).at[slot_table].add(row_grad)[:seq_len]
    weight_grad_tok = (
        jnp.zeros((seq_len + 1, local_count), single)
        .at[slot_table, expert_cols]
        .add(slot_weight_grad)[:seq_len]
    )
    route_grad = jnp.sum(weight_grad_tok[:, None, :] * chosen_float, axis=-1)
    logit_part = gating * (route_grad - jnp.sum(gating * route_grad, axis=-1, keepdims=True))
    normed_two_grad, logits_rows = (
        lax.psum_scatter(normed_two_part, "seq", scatter_dimension=0, tiled=True),
        lax.psum_scatter(logit_part, "seq", scatter_dimension=0, tiled=True),
    )
    gate_term = jnp.einsum("ecd,ecf->def", slot_rows, gate_grad_low, preferred_element_type=single)
    up_term = jnp.einsum("ecd,ecf->def", slot_rows, up_grad_low, preferred_element_type=single)
    down_term = jnp.einsum("ecd,ecf->def", out_low, mid_low, preferred_element_type=single)
    expert_total = lax.psum_scatter(
        jnp.concatenate([gate_term, up_term, down_term], 2).astype(jnp.bfloat16),
        "fsdp",
        scatter_dimension=0,
        tiled=True,
    ).astype(jnp.float32)
    unused, norm_two_back = jax.vjp(norm_apply, hidden, gains_float[:, 1])
    hidden_part, gain_two_grad = norm_two_back(normed_two_grad)
    hidden_grad = cotangent[0].astype(single) + hidden_part
    attn_grad_low = hidden_grad.astype(narrow)
    attended_grad = jnp.dot(attn_grad_low, exit_full, preferred_element_type=single).astype(narrow)
    grads_heads = lax.all_to_all(attended_grad, "seq", split_axis=1, concat_axis=0, tiled=True)
    grad_blocks = grads_heads.reshape(blocks, QBLK, local_kv, group_size, HEAD_DIM)

    def attend_back(carried, block_items):
        keys_sum, values_sum = carried
        row_block, grad_block, block_log, first_row = block_items
        scores = block_scores(row_block, first_row)
        soft_float = jnp.exp(scores - block_log[..., None])
        soft_weights = soft_float.astype(narrow)
        values_sum = values_sum + jnp.einsum(
            "kgbt,bkgd->tkd", soft_weights, grad_block, preferred_element_type=single
        )
        soft_grad = jnp.einsum(
            "bkgd,tkd->kgbt", grad_block, value_heads, preferred_element_type=single
        )
        row_delta = jnp.sum(soft_float * soft_grad, axis=-1, keepdims=True)
        scores_grad = (soft_float * (soft_grad - row_delta)).astype(narrow)
        query_grad = (
            jnp.einsum("kgbt,tkd->bkgd", scores_grad, key_heads, preferred_element_type=single)
            * score_scale
        )
        keys_sum = (
            keys_sum
            + jnp.einsum("kgbt,bkgd->tkd", scores_grad, row_block, preferred_element_type=single)
            * score_scale
        )
        return ((keys_sum, values_sum), query_grad.astype(narrow))

    zero_heads = jnp.zeros((seq_len, local_kv, HEAD_DIM), single)
    (keys_sum, values_sum), query_grads = lax.scan(
        attend_back, (zero_heads, zero_heads), (query_blocks, grad_blocks, log_totals, starts)
    )
    query_send_grad = query_grads.reshape(seq_len, -1)
    key_send_grad = keys_sum.reshape(seq_len, -1).astype(narrow)
    value_send_grad = values_sum.reshape(seq_len, -1).astype(narrow)
    query_back, key_back, value_back = (
        lax.all_to_all(query_send_grad, "seq", split_axis=0, concat_axis=1, tiled=True),
        lax.all_to_all(key_send_grad, "seq", split_axis=0, concat_axis=1, tiled=True),
        lax.all_to_all(value_send_grad, "seq", split_axis=0, concat_axis=1, tiled=True),
    )

    def turn_rows(entries):
        return rotate(entries, cos_table, sin_table)

    unused, query_turn_back = jax.vjp(turn_rows, query_raw)
    unused, key_turn_back = jax.vjp(turn_rows, key_raw)
    query_raw_grad = query_turn_back(query_back.astype(single).reshape(tok_rows, HEADS, HEAD_DIM))[
        0
    ]
    key_raw_grad = key_turn_back(key_back.astype(single).reshape(tok_rows, KV_HEADS, HEAD_DIM))[0]
    projected_grad = jnp.concatenate(
        [
            query_raw_grad.reshape(tok_rows, query_width).astype(narrow),
            key_raw_grad.reshape(tok_rows, key_width).astype(narrow),
            value_back,
        ],
        1,
    )
    normed_grad = lax.dot_general(
        projected_grad, mixing_full, (((1,), (1,)), ((), ())), preferred_element_type=single
    )
    unused, norm_one_back = jax.vjp(norm_apply, inputs, gains_float[:, 0])
    input_part, gain_one_grad = norm_one_back(normed_grad)
    tokens_gradient = (hidden_grad + input_part)[None]
    gains_term = jnp.stack([gain_one_grad, gain_two_grad], 1)
    mixing_term = lax.dot_general(
        normed_low, projected_grad, (((0,), (0,)), ((), ())), preferred_element_type=single
    )
    output_term = lax.dot_general(
        attn_grad_low, attn_rows, (((0,), (0,)), ((), ())), preferred_element_type=single
    )
    attn_total = lax.psum_scatter(
        jnp.concatenate([mixing_term, output_term, gains_term], 1),
        ("seq", "fsdp"),
        scatter_dimension=0,
        tiled=True,
    )
    mixing_gradient = attn_total[:, :mixing_width]
    output_gradient = attn_total[:, mixing_width : mixing_width + query_width]
    gains_gradient = attn_total[:, mixing_width + query_width :]
    gate_gradient = expert_total[:, :, :FF]
    up_gradient = expert_total[:, :, FF : 2 * FF]
    down_gradient = expert_total[:, :, 2 * FF :]
    return (
        layer_output,
        tokens_gradient,
        mixing_gradient,
        output_gradient,
        gains_gradient,
        gate_gradient,
        up_gradient,
        down_gradient,
        logits_rows[None],
    )


def solution(mesh):
    in_specs = (
        P("fsdp", "seq", None),
        P(("seq", "fsdp"), None),
        P(("seq", "fsdp"), None),
        P(("seq", "fsdp"), None),
        P("fsdp", "seq", None),
        P("fsdp", "seq", None),
        P("fsdp", "seq", None),
        P("fsdp", None, None),
        P("fsdp", None, None),
        P("fsdp", None),
        P("fsdp", "seq", None),
    )
    out_specs = (
        P("fsdp", "seq", None),
        P("fsdp", "seq", None),
        P(("seq", "fsdp"), None),
        P(("seq", "fsdp"), None),
        P(("seq", "fsdp"), None),
        P("fsdp", "seq", None),
        P("fsdp", "seq", None),
        P("fsdp", "seq", None),
        P("fsdp", "seq", None),
    )
    return jax.shard_map(local, mesh=mesh, in_specs=in_specs, out_specs=out_specs, check_vma=False)
```

profile of v0, /device:TPU:0, one launch (start us, length us, event | category | flops | bytes accessed | tf_op | source)
XLA Modules:
  0.0 1854.2 jit_solution(63584453304176128)
XLA Ops:
  8.7 43.3 %all-gather.1 = bf16[32,48,2]{1,2,0:T(2,128)(2,1)S(1)} all-gather(bf16[1,48,2]{1,2,0:T(2,128)(2,1)} %bitcast.352), channel_id=1, replica_groups=mesh['seq'=4,'fsdp'=8] {'seq','fsdp'}, dimensions={0}, use_global_device_ids=true | all-gather | bytes 6336 | tf_op jit(solution)/shard_map/all_gather | solution.py:94
  57.3 32.0 %all-gather.10.cloned.1.call-done = bf16[1536,2560]{1,0:T(8,128)(2,1)} async-done(((bf16[48,2560]{1,0:T(8,128)(2,1)}), bf16[1536,2560]{1,0:T(8,128)(2,1)}) %all-gather.10.cloned.1.call-update) | async-done | bytes 7864336 | tf_op jit(solution)/shard_map/all_gather | solution.py:92
  131.2 12.9 all-to-all-done
  147.4 23.8 %while.28 = (s32[]{:T(128)}, bf16[2,512,2,3,64]{1,4,3,2,0:T(8,128)(2,1)S(1)}, f32[2,2,3,512]{3,2,1,0:T(4,128)S(1)}, s32[2]{0:T(128)S(1)}, bf16[2,512,2,3,64]{1,4...) while((s32[]{:T(128)}, ...), condition=%wide.region_4.5_spmd.clone, body=%wide.region_1.4_spmd.clone.sunk | while | flops 843773440 | bytes 41279608 | solution.py:144
  180.1 12.1 all-to-all-done.3
  213.5 37.9 %scatter_custom_fusion.3 = s32[2060]{0:T(1024)S(1)} fusion(s32[10240]{0:T(1024)S(1)} %reshape.356, s32[10240]{0:T(1024)S(1)} %reshape.358, s32[]{:T(128)} %constant.52.clone.1), kind=kCustom, calls=%fused_computation.179 | custom fusion | bytes 8244
  254.8 8.5 gather_fusion.3
  263.3 11.4 reshape.378
  276.8 8.5 gather_fusion.1
  285.3 8.8 reshape.311
  294.1 101.2 %all-gather.16.cloned.1.call-done = bf16[1536,10,512]{2,0,1:T(8,128)(2,1)} async-done(((bf16[192,10,512]{2,0,1:T(8,128)(2,1)}), bf16[1536,10,512]{2,0,1:T(8,128)(2,1)}) %all-gather.16.cloned.1.call-update) | async-done | bytes 15728656 | tf_op jit(solution)/shard_map/all_gather | solution.py:165
  395.3 13.3 fusion.103
  408.6 128.9 %all-gather.18.cloned.1.call-done = bf16[1536,10,512]{2,0,1:T(8,128)(2,1)} async-done(((bf16[192,10,512]{2,0,1:T(8,128)(2,1)}), bf16[1536,10,512]{2,0,1:T(8,128)(2,1)}) %all-gather.18.cloned.1.call-update) | async-done | bytes 15728656 | tf_op jit(solution)/shard_map/all_gather | solution.py:166
  537.5 15.1 multiply_convert_fusion.3
  552.6 127.2 %all-gather.20.cloned.1.call-done = bf16[1536,10,512]{2,0,1:T(8,128)(2,1)} async-done(((bf16[192,10,512]{2,0,1:T(8,128)(2,1)}), bf16[1536,10,512]{2,0,1:T(8,128)(2,1)}) %all-gather.20.cloned.1.call-update) | async-done | bytes 15728656 | tf_op jit(solution)/shard_map/all_gather | solution.py:167
  679.8 15.5 multiply_reduce_fusion
  695.4 16.0 scatter_custom_fusion.4
  712.6 19.8 %gather_fusion.2 = f32[2050]{0:T(1024)S(1)} fusion(f32[1025,10]{1,0:T(8,128)S(1)} %concatenate.44, s32[2050]{0:T(1024)S(1)} %reshape.318), kind=kCustom, calls=%fused_computation.2 | custom fusion | bytes 32800 | tf_op jit(solution)/shard_map/gather | solution.py:161
  732.5 15.0 multiply_convert_fusion.1
  747.5 12.8 fusion.104
  760.3 15.0 convolution_add_fusion
  775.3 12.5 reshape.352
  787.8 29.5 %scatter_custom_fusion.2 = f32[1025,1536]{1,0:T(8,128)} fusion(s32[2050]{0:T(1024)S(1)} %reshape.342, f32[2050,1536]{1,0:T(8,128)} %reshape.352, f32[]{:T(128)} %constant.30.clone.1), kind=kCustom, calls=%fused_computation.87 | custom fusion | flops 3148800 | bytes 6298112 | tf_op jit(solution)/shard_map/scatter-add | solution.py:202
  817.4 5.9 slice.109
  823.4 10.2 broadcast_multiply_fusion
  833.5 13.2 reshape.344
  846.7 29.4 %scatter_custom_fusion.1 = f32[1025,1536]{1,0:T(8,128)} fusion(s32[2050]{0:T(1024)S(1)} %reshape.342, f32[2050,1536]{1,0:T(8,128)} %reshape.344, f32[]{:T(128)} %constant.30.clone.1), kind=kCustom, calls=%fused_computation.89 | custom fusion | flops 3148800 | bytes 6298112 | tf_op jit(solution)/shard_map/scatter-add | solution.py:177
  881.1 10.8 reduce-scatter.10.cloned.1.call-done
  894.3 45.2 %reduce-scatter.8.cloned.1.call-done = bf16[256,1536]{1,0:T(8,128)(2,1)} async-done(((bf16[1024,1536]{1,0:T(8,128)(2,1)}), bf16[256,1536]{1,0:T(8,128)(2,1)}) %reduce-scatter.8.cloned.1.call-update) | async-done | bytes 786448 | tf_op jit(solution)/shard_map/reduce_scatter | solution.py:179
  952.3 11.0 all-to-all-done.4
  966.4 56.4 %while.29 = (s32[]{:T(128)}, f32[1024,2,64]{0,2,1:T(8,128)S(1)}, f32[1024,2,64]{0,2,1:T(8,128)}, bf16[2,512,2,3,64]{1,4,3,2,0:T(8,128)(2,1)}, bf16[2,512,2,3,64]...) while((s32[]{:T(128)}, f32[1024,2,64]{0,2,1:T(8,128)S(1)}, ...), condition=%wide.region_21.22_spmd.clone, body=%wide.region_19.21_spmd.clone.sunk | while | flops 2062022144 | bytes 184250800 | solution.py:257
  970.0 5.7 fusion.160
  985.0 6.6 fusion.163
  1013.2 6.6 fusion.163
  1027.4 6.7 fusion.75
  1042.8 9.5 all-to-all-done.5
  1061.1 7.9 fusion.72
  1069.0 6.8 fusion.65
  1076.1 27.7 %concatenate.48 = f32[1536,4098]{1,0:T(8,128)} concatenate(f32[1536,2560]{1,0:T(8,128)} %fusion.72, f32[1536,1536]{1,0:T(8,128)} %fusion.75, f32[1536,1]{1,0:T(8,128)S(1)} %stack.8, f32[1536,1]{1,0:T(8,128)S(1)} %copy-done.25), dimensions={1} | concatenate | bytes 50356224 | tf_op jit(solution)/shard_map/concatenate | solution.py:300
  1105.4 12.4 convert_bitcast_fusion.1
  1117.8 12.8 convert_bitcast_fusion.2
  1130.6 15.1 convert_bitcast_fusion
  1145.7 35.1 %pad_maximum_fusion = bf16[1536,10,1536]{0,2,1:T(8,128)(2,1)} fusion(bf16[1536,10,512]{0,2,1:T(8,128)(2,1)} %convert_bitcast_fusion, bf16[1536,10,512]{0,2,1:T(8,128)(2,1)} %convert_bitcast_fusion.1, bf16[1536,10,512]{0,2,1:T(8,128)(2,1)} %convert_bitcast_fusion.2), kind=kLoop, calls=%fused_computation.74 | loop fusion | flops 141557760 | bytes 94371840 | tf_op jit(solution)/shard_map/concatenate | solution.py:218
  1180.8 57.6 %copy.314 = bf16[1536,15360]{1,0:T(8,128)(2,1)} copy(bf16[1536,15360]{0,1:T(8,128)(2,1)} %bitcast.320) | data formatting | bytes 94371840
  1242.9 112.8 %reduce-scatter.12.cloned.1.call-done = f32[48,4098]{1,0:T(8,128)} async-done(((f32[1536,4098]{1,0:T(8,128)}), f32[48,4098]{1,0:T(8,128)}) %reduce-scatter.12.cloned.1.call-update) | async-done | bytes 786832 | tf_op jit(solution)/shard_map/reduce_scatter | solution.py:299
  1360.7 450.7 %reduce-scatter.16.cloned.1.call-done = bf16[192,15360]{1,0:T(8,128)(2,1)} async-done(((bf16[1536,15360]{1,0:T(8,128)(2,1)}), bf16[192,15360]{1,0:T(8,128)(2,1)}) %reduce-scatter.16.cloned.1.call-update) | async-done | bytes 5898256
  1811.3 9.7 copy.315
  1821.0 9.3 fusion.100
  (362 shorter events, 222.0 us)
Async XLA Ops:
  7.2 49.8 %copy-start.17 = (bf16[1,256,1536]{2,1,0:T(8,128)(2,1)S(1)}, bf16[1,256,1536]{2,1,0:T(8,128)(2,1)}, u32[]{:S(2)}) copy-start(bf16[1,256,1536]{2,1,0:T(8,128)(2,1)} %param.15) | copy-start | bytes 2359300
  7.2 82.1 %all-gather.10.cloned.1.call-start = ((), (), s32[]{:S(2)}) async-start(), calls=%async_computation.13 | async-start | bytes 8110080 | tf_op jit(solution)/shard_map/all_gather | solution.py:92
  7.9 172.2 %all-gather.12.cloned.1.call-start = ((), (), s32[]{:S(2)}) async-start(), calls=%async_computation.14 | async-start | bytes 4866048 | tf_op jit(solution)/shard_map/all_gather | solution.py:93
  52.3 42.5 %copy-start.26 = (f32[256,64]{0,1:T(8,128)}, f32[256,64]{0,1:T(8,128)S(1)}, u32[]{:S(2)}) copy-start(f32[256,64]{0,1:T(8,128)S(1)} %get-tuple-element.430) | copy-start | bytes 196612
  52.3 53.7 %copy-start.28 = (f32[256,64]{0,1:T(8,128)}, f32[256,64]{0,1:T(8,128)S(1)}, u32[]{:S(2)}) copy-start(f32[256,64]{0,1:T(8,128)S(1)} %get-tuple-element.431) | copy-start | bytes 196612
  57.0 37.8 %copy-start.36 = (f32[1536]{0:T(1024)}, f32[1536]{0:T(1024)S(1)}, u32[]{:S(2)}) copy-start(f32[1536]{0:T(1024)S(1)} %get-tuple-element.365) | copy-start | bytes 18436
  57.0 140.0 %copy-start.42 = (f32[1536]{0:T(1024)}, f32[1536]{0:T(1024)S(1)}, u32[]{:S(2)}) copy-start(f32[1536]{0:T(1024)S(1)} %get-tuple-element.364) | copy-start | bytes 18436
  57.2 37.6 %copy-start.54 = (f32[256]{0:T(256)}, f32[256]{0:T(256)S(1)}, u32[]{:S(2)}) copy-start(f32[256]{0:T(256)S(1)} %fusion.69) | copy-start | bytes 3076
  57.2 37.6 %copy-start.50 = (f32[256]{0:T(256)}, f32[256]{0:T(256)S(1)}, u32[]{:S(2)}) copy-start(f32[256]{0:T(256)S(1)} %fusion.95) | copy-start | bytes 3076
  108.1 9.4 all-to-all-start.1
  117.5 8.8 all-to-all-start.2
  126.2 17.9 all-to-all-start
  129.7 122.4 %all-gather.22.cloned.1.call-start = ((), (), s32[]{:S(2)}) async-start(), calls=%async_computation.23 | async-start | bytes 3932160 | tf_op jit(solution)/shard_map/all_gather | solution.py:183
  171.2 25.2 %copy-start.1 = (bf16[1024,2,64]{0,2,1:T(8,128)(2,1)}, bf16[1024,2,64]{0,2,1:T(8,128)(2,1)S(1)}, u32[]{:S(2)}) copy-start(bf16[1024,2,64]{0,2,1:T(8,128)(2,1)S(1)} %get-tuple-element.621) | copy-start | bytes 786436
  171.2 25.2 %copy-start.3 = (bf16[2,512,2,3,64]{1,4,3,2,0:T(8,128)(2,1)}, bf16[2,512,2,3,64]{1,4,3,2,0:T(8,128)(2,1)S(1)}, u32[]{:S(2)}) copy-start(bf16[2,512,2,3,64]{1,4,3,2,0:T(8,128)(2,1)S(1)} %get-tuple-element.622) | copy-start | bytes 2359300
  171.2 25.2 %copy-start.16 = (bf16[1024,2,64]{0,2,1:T(8,128)(2,1)}, bf16[1024,2,64]{0,2,1:T(8,128)(2,1)S(1)}, u32[]{:S(2)}) copy-start(bf16[1024,2,64]{0,2,1:T(8,128)(2,1)S(1)} %get-tuple-element.629) | copy-start | bytes 786436
  171.2 25.2 %copy-start.38 = (f32[2,2,3,512]{3,2,1,0:T(4,128)}, f32[2,2,3,512]{3,2,1,0:T(4,128)S(1)}, u32[]{:S(2)}) copy-start(f32[2,2,3,512]{3,2,1,0:T(4,128)S(1)} %get-tuple-element.575) | copy-start | bytes 73732
  171.2 25.2 %copy-start.63 = (s32[2]{0:T(128)}, s32[2]{0:T(128)S(1)}, u32[]{:S(2)}) copy-start(s32[2]{0:T(128)S(1)} %get-tuple-element.663) | copy-start | bytes 28
  176.5 15.7 all-to-all-start.3
  180.0 94.7 %all-gather.14.cloned.1.call-start = ((), (), s32[]{:S(2)}) async-start(), calls=%async_computation.15 | async-start | bytes 3932160 | tf_op jit(solution)/shard_map/all_gather | solution.py:153
  198.7 196.6 %all-gather.16.cloned.1.call-start = ((), (), s32[]{:S(2)}) async-start(), calls=%async_computation.16 | async-start | bytes 17694720 | tf_op jit(solution)/shard_map/all_gather | solution.py:165
  199.3 338.2 %all-gather.18.cloned.1.call-start = ((), (), s32[]{:S(2)}) async-start(), calls=%async_computation.17 | async-start | bytes 17694720 | tf_op jit(solution)/shard_map/all_gather | solution.py:166
  199.8 480.0 %all-gather.20.cloned.1.call-start = ((), (), s32[]{:S(2)}) async-start(), calls=%async_computation.18 | async-start | bytes 17694720 | tf_op jit(solution)/shard_map/all_gather | solution.py:167
  200.6 691.3 %reduce-scatter.10.cloned.1.call-start = ((), (), s32[]{:S(2)}) async-start(), calls=%async_computation.20 | async-start | bytes 7864320 | tf_op jit(solution)/shard_map/reduce_scatter | solution.py:211
  204.4 47.2 %copy-start.60 = (s32[2]{0:T(128)S(1)}, s32[2]{0:T(128)}, u32[]{:S(2)}) copy-start(s32[2]{0:T(128)} %constant.133) | copy-start | bytes 28
  204.4 47.3 %copy-start.59 = (s32[2]{0:T(128)S(1)}, s32[2]{0:T(128)}, u32[]{:S(2)}) copy-start(s32[2]{0:T(128)} %constant.136) | copy-start | bytes 28
  204.4 47.6 %copy-start.30 = (f32[1,1024,8]{1,2,0:T(8,128)S(1)}, f32[1,1024,8]{1,2,0:T(8,128)}, u32[]{:S(2)}) copy-start(f32[1,1024,8]{1,2,0:T(8,128)} %param.22) | copy-start | bytes 98308
  552.6 142.8 %copy-start.5 = (bf16[10,205,512]{2,1,0:T(8,128)(2,1)}, bf16[10,205,512]{2,1,0:T(8,128)(2,1)S(1)}, u32[]{:S(2)}) copy-start(bf16[10,205,512]{2,1,0:T(8,128)(2,1)S(1)} %get-tuple-element.425) | copy-start | bytes 6297604
  732.5 90.9 %copy-start.40 = (f32[10,205]{1,0:T(8,128)}, f32[10,205]{1,0:T(8,128)S(1)}, u32[]{:S(2)}) copy-start(f32[10,205]{1,0:T(8,128)S(1)} %reshape.321) | copy-start | bytes 24604
  823.3 116.2 %reduce-scatter.8.cloned.1.call-start = ((), (), s32[]{:S(2)}) async-start(), calls=%async_computation.19 | async-start | bytes 3932160 | tf_op jit(solution)/shard_map/reduce_scatter | solution.py:179
  876.2 15.8 copy-start.14
  876.2 15.8 copy-start.43
  876.2 15.8 copy-start.53
  881.1 13.2 copy-start.57
  881.1 58.4 %copy-start.20 = (bf16[1,256,1536]{2,1,0:T(8,128)(2,1)S(1)}, bf16[1,256,1536]{2,1,0:T(8,128)(2,1)}, u32[]{:S(2)}) copy-start(bf16[1,256,1536]{2,1,0:T(8,128)(2,1)} %param.25) | copy-start | bytes 2359300
  947.4 19.0 %copy-start.2 = (bf16[1024,2,64]{0,2,1:T(8,128)(2,1)S(1)}, bf16[1024,2,64]{0,2,1:T(8,128)(2,1)}, u32[]{:S(2)}) copy-start(bf16[1024,2,64]{0,2,1:T(8,128)(2,1)} %copy-done.1) | copy-start | bytes 786436
  947.4 19.0 %copy-start.4 = (bf16[2,512,2,3,64]{1,4,3,2,0:T(8,128)(2,1)S(1)}, bf16[2,512,2,3,64]{1,4,3,2,0:T(8,128)(2,1)}, u32[]{:S(2)}) copy-start(bf16[2,512,2,3,64]{1,4,3,2,0:T(8,128)(2,1)} %copy-done.3) | copy-start | bytes 2359300
  947.4 19.0 %copy-start.39 = (f32[2,2,3,512]{3,2,1,0:T(4,128)S(1)}, f32[2,2,3,512]{3,2,1,0:T(4,128)}, u32[]{:S(2)}) copy-start(f32[2,2,3,512]{3,2,1,0:T(4,128)} %copy-done.38) | copy-start | bytes 73732
  947.4 19.0 %copy-start.64 = (s32[2]{0:T(128)S(1)}, s32[2]{0:T(128)}, u32[]{:S(2)}) copy-start(s32[2]{0:T(128)} %copy-done.63) | copy-start | bytes 28
  948.6 14.7 all-to-all-start.4
  1023.7 14.7 all-to-all-start.6
  1038.4 14.0 all-to-all-start.5
  1052.4 8.8 all-to-all-start.7
  1055.8 300.0 %reduce-scatter.12.cloned.1.call-start = ((), (), s32[]{:S(2)}) async-start(), calls=%async_computation.21 | async-start | bytes 26763264 | tf_op jit(solution)/shard_map/reduce_scatter | solution.py:299
  1103.8 707.6 %reduce-scatter.16.cloned.1.call-start = ((), (), s32[]{:S(2)}) async-start(), calls=%async_computation.24 | async-start | bytes 53084160
  1117.7 12.8 copy-start.6
  1117.7 12.8 copy-start.41
  1238.4 608.5 %reduce-scatter.14.cloned.1.call-start = ((), (), s32[]{:S(2)}) async-start(), calls=%async_computation.22 | async-start | bytes 40960 | tf_op jit(solution)/shard_map/reduce_scatter | solution.py:212
  (48 other events, 239.1 us)
Sparse Core Ops, SparseCore 0:
  11.0 78.1 all-gather.9
  92.3 64.7 all-gather.11
  158.9 46.2 all-gather.21
  207.5 43.7 all-gather.13
  252.7 142.5 all-gather.15
  396.7 140.6 all-gather.17
  539.1 140.6 all-gather.19
  823.4 68.4 reduce-scatter.9
  895.5 43.9 reduce-scatter.7
  1103.9 251.8 reduce-scatter.11
  1358.1 453.1 reduce-scatter.15
  1814.5 21.9 reduce-scatter.13
where the time goes:
time: 1860 us; the launch traced here: 1850 us
  waiting for transfers between devices  1070 us (58%)
  local copies, waits for them, and re-layouts  315 us (17%)
  matrix products  216 us (12%)
  other arithmetic  165 us (9%)
  blocking collectives  43.3 us (2%)
  starting transfers between devices  29.8 us (2%)
    unnamed x13, waiting for transfers between devices  454 us
    unnamed x131, local copies, waits for them, and re-layouts  131 us
    all_gather x1, waiting for transfers between devices, local(): lax.all_gather(expert_up, 'fsdp', axis=0, tiled=True)  129 us
    all_gather x1, waiting for transfers between devices, local(): lax.all_gather(expert_down, 'fsdp', axis=0, tiled=True)  127 us
    reduce_scatter x1, waiting for transfers between devices, local(): lax.psum_scatter(jnp.concatenate([mixing_term, output_term, gains_term],...  113 us
    all_gather x1, waiting for transfers between devices, local(): lax.all_gather(expert_gate, 'fsdp', axis=0, tiled=True)  101 us
    reduce_scatter x1, waiting for transfers between devices, local(): lax.psum_scatter(partial_sum.astype(jnp.bfloat16), 'seq', scatter_dimensi...  45.2 us
    all_gather x1, blocking collectives, local(): lax.all_gather(norm_gains, ('seq', 'fsdp'), axis=0, tiled=True)  43.3 us
  transfers between devices with their start and end apart: 20, of which 15 were waited for; matrix products, arithmetic and copies ran while one was open for 23% of the time, Pallas kernels for 0%

commit v1 on v0

--- a/solution.py
+++ b/solution.py
@@ -14,6 +14,19 @@
 QBLK = 512
 epsilon = 1e-05
 rope_base = 10000.0
+
+
+def ring_gather(array, axis, dim):
+    ways = lax.axis_size(axis)
+    up = [(d, (d + 1) % ways) for d in range(ways)]
+    down = [(d, (d - 1) % ways) for d in range(ways)]
+    earlier, later = ([array], [array])
+    for _ in range(ways // 2):
+        earlier.append(lax.ppermute(earlier[-1], axis, up))
+    for _ in range((ways - 1) // 2):
+        later.append(lax.ppermute(later[-1], axis, down))
+    line = jnp.concatenate([*earlier[::-1], *later[1:]], axis=dim)
+    return jnp.roll(line, (lax.axis_index(axis) - ways // 2) * array.shape[dim], axis=dim)
 
 
 def norm_apply(values, gain_row):
@@ -162,7 +175,7 @@
     padded_rows = jnp.concatenate([seq_rows, jnp.zeros((1, D), narrow)], 0)
     slot_rows = padded_rows[slot_table]
     gate_full, up_full, down_full = (
-        lax.all_gather(expert_gate, "fsdp", axis=0, tiled=True),
+        ring_gather(expert_gate, "fsdp", 0),
         lax.all_gather(expert_up, "fsdp", axis=0, tiled=True),
         lax.all_gather(expert_down, "fsdp", axis=0, tiled=True),
     )

time: 1860 us -> 1880 us (1.011)
  local copies, waits for them, and re-layouts: 315 us -> 357 us
  waiting for transfers between devices: 1070 us -> 1030 us
    ppermute x0 -> x7, waiting for transfers between devices: none -> 176 us  [the longest x4 149 us: ring_gather(): earlier.append(lax.ppermute(earlier[-1], axis, up))]
    all_gather x1, waiting for transfers between devices: 129 us -> 0.01 us  [local(): lax.all_gather(expert_up, 'fsdp', axis=0, tiled=True)]
    all_gather x1, waiting for transfers between devices: 127 us -> 73.5 us  [local(): lax.all_gather(expert_down, 'fsdp', axis=0, tiled=True)]
    unnamed x131 -> x154, local copies, waits for them, and re-layouts: 131 us -> 171 us
    all_gather x1, waiting for transfers between devices: 101 us -> 70.6 us  [local(): lax.all_gather(expert_gate, 'fsdp', axis=0, tiled=True)]
  transfers between devices with their start and end apart: 20 -> 27, of which waited for: 15 -> 20; matrix products, arithmetic and copies ran while one was open for 23% -> 29% of each run, Pallas kernels for 0% -> 0%
where the time goes in v1:
time: 1880 us; the launch traced here: 1870 us
  waiting for transfers between devices  1030 us (55%)
  local copies, waits for them, and re-layouts  357 us (19%)
  matrix products  218 us (12%)
  other arithmetic  165 us (9%)
  blocking collectives  43.3 us (2%)
  starting transfers between devices  41 us (2%)
    unnamed x13, waiting for transfers between devices  454 us
    unnamed x154, local copies, waits for them, and re-layouts  171 us
    ppermute x4, waiting for transfers between devices, ring_gather(): earlier.append(lax.ppermute(earlier[-1], axis, up))  149 us
    reduce_scatter x1, waiting for transfers between devices, local(): lax.psum_scatter(jnp.concatenate([mixing_term, output_term, gains_term],...  113 us
    all_gather x1, waiting for transfers between devices, local(): lax.all_gather(expert_down, 'fsdp', axis=0, tiled=True)  73.5 us
    all_gather x1, waiting for transfers between devices, local(): lax.all_gather(expert_gate, 'fsdp', axis=0, tiled=True)  70.6 us
    reduce_scatter x1, waiting for transfers between devices, local(): lax.psum_scatter(partial_sum.astype(jnp.bfloat16), 'seq', scatter_dimensi...  45.2 us
    all_gather x1, blocking collectives, local(): lax.all_gather(norm_gains, ('seq', 'fsdp'), axis=0, tiled=True)  43.3 us
  transfers between devices with their start and end apart: 27, of which 20 were waited for; matrix products, arithmetic and copies ran while one was open for 29% of the time, Pallas kernels for 0%

profile of v1, /device:TPU:0, one launch (start us, length us, event | category | flops | bytes accessed | tf_op | source)
XLA Modules:
  0.0 1871.8 jit_solution(142029690949257419)
XLA Ops:
  8.7 43.3 %all-gather.1 = bf16[32,48,2]{1,2,0:T(2,128)(2,1)S(1)} all-gather(bf16[1,48,2]{1,2,0:T(2,128)(2,1)} %bitcast.351), channel_id=1, replica_groups=mesh['seq'=4,'fsdp'=8] {'seq','fsdp'}, dimensions={0}, use_global_device_ids=true | all-gather | bytes 6336 | tf_op jit(solution)/shard_map/all_gather | solution.py:107
  57.3 32.0 %all-gather.10.cloned.1.call-done = bf16[1536,2560]{1,0:T(8,128)(2,1)} async-done(((bf16[48,2560]{1,0:T(8,128)(2,1)}), bf16[1536,2560]{1,0:T(8,128)(2,1)}) %all-gather.10.cloned.1.call-update) | async-done | bytes 7864336 | tf_op jit(solution)/shard_map/all_gather | solution.py:105
  131.2 12.9 all-to-all-done
  147.5 23.8 %while.28 = (s32[]{:T(128)}, bf16[2,512,2,3,64]{1,4,3,2,0:T(8,128)(2,1)S(1)}, f32[2,2,3,512]{3,2,1,0:T(4,128)S(1)}, s32[2]{0:T(128)S(1)}, bf16[2,512,2,3,64]{1,4...) while((s32[]{:T(128)}, ...), condition=%wide.region_4.5_spmd.clone, body=%wide.region_1.4_spmd.clone.sunk | while | flops 843773440 | bytes 41279608 | solution.py:157
  180.2 12.3 all-to-all-done.3
  201.5 25.8 %collective-permute-done = bf16[192,10,512]{2,0,1:T(8,128)(2,1)S(1)} collective-permute-done((bf16[192,10,512]{2,0,1:T(8,128)(2,1)S(1)}, bf16[192,10,512]{2,0,1:T(8,128)(2,1)S(1)}, u32[]{:S(2)}, u32[]{:S(2)}) %collective-permute-start) | collective-permute-done | bytes 1966112 | tf_op jit(solution)/shard_map/ppermute | solution.py:25
  230.9 50.2 %collective-permute-done.1 = bf16[192,10,512]{2,0,1:T(8,128)(2,1)} collective-permute-done((bf16[192,10,512]{2,0,1:T(8,128)(2,1)S(1)}, bf16[192,10,512]{2,0,1:T(8,128)(2,1)}, u32[]{:S(2)}, u32[]{:S(2)}) %collective-permute-start.1) | collective-permute-done | bytes 1966112 | tf_op jit(solution)/shard_map/ppermute | solution.py:25
  299.1 70.2 %collective-permute-done.2 = bf16[192,10,512]{2,0,1:T(8,128)(2,1)} collective-permute-done((bf16[192,10,512]{2,0,1:T(8,128)(2,1)}, bf16[192,10,512]{2,0,1:T(8,128)(2,1)}, u32[]{:S(2)}, u32[]{:S(2)}) %collective-permute-start.2) | collective-permute-done | bytes 1966112 | tf_op jit(solution)/shard_map/ppermute | solution.py:25
  371.1 37.9 %scatter_custom_fusion.3 = s32[2060]{0:T(1024)S(1)} fusion(s32[10240]{0:T(1024)S(1)} %reshape.356, s32[10240]{0:T(1024)S(1)} %reshape.358, s32[]{:T(128)} %constant.70.clone.1), kind=kCustom, calls=%fused_computation.197 | custom fusion | bytes 8244
  416.0 8.4 gather_fusion.3
  424.4 10.5 reshape.378
  455.5 23.7 %collective-permute-done.6 = bf16[192,10,512]{2,0,1:T(8,128)(2,1)} collective-permute-done((bf16[192,10,512]{2,0,1:T(8,128)(2,1)}, bf16[192,10,512]{2,0,1:T(8,128)(2,1)}, u32[]{:S(2)}, u32[]{:S(2)}) %collective-permute-start.6) | collective-permute-done | bytes 1966112 | tf_op jit(solution)/shard_map/ppermute | solution.py:27
  505.3 8.4 gather_fusion.1
  513.7 9.1 reshape.311
  522.8 13.2 fusion.57
  536.0 14.4 multiply_convert_fusion.3
  550.4 73.5 %all-gather.18.cloned.1.call-done = bf16[1536,10,512]{2,0,1:T(8,128)(2,1)} async-done(((bf16[192,10,512]{2,0,1:T(8,128)(2,1)}), bf16[1536,10,512]{2,0,1:T(8,128)(2,1)}) %all-gather.18.cloned.1.call-update) | async-done | bytes 15728656 | tf_op jit(solution)/shard_map/all_gather | solution.py:180
  623.9 18.0 multiply_reduce_fusion
  642.0 16.0 scatter_custom_fusion.4
  659.1 20.2 %gather_fusion.2 = f32[2050]{0:T(1024)S(1)} fusion(f32[1025,10]{1,0:T(8,128)S(1)} %concatenate.51, s32[2050]{0:T(1024)S(1)} %reshape.318), kind=kCustom, calls=%fused_computation.2 | custom fusion | bytes 32800 | tf_op jit(solution)/shard_map/gather | solution.py:174
  679.4 16.2 multiply_convert_fusion.1
  695.6 70.6 %all-gather.20.cloned.1.call-done = bf16[1536,10,512]{2,0,1:T(8,128)(2,1)} async-done(((bf16[192,10,512]{2,0,1:T(8,128)(2,1)}), bf16[1536,10,512]{2,0,1:T(8,128)(2,1)}) %all-gather.20.cloned.1.call-update) | async-done | bytes 15728656 | tf_op jit(solution)/shard_map/all_gather | solution.py:202
  766.2 11.1 fusion.106
  777.3 16.0 convolution_add_fusion
  793.3 12.4 reshape.352
  805.7 29.5 %scatter_custom_fusion.2 = f32[1025,1536]{1,0:T(8,128)} fusion(s32[2050]{0:T(1024)} %copy-done.52, f32[2050,1536]{1,0:T(8,128)} %reshape.352, f32[]{:T(128)} %constant.57.clone.1), kind=kCustom, calls=%fused_computation.89 | custom fusion | flops 3148800 | bytes 6298112 | tf_op jit(solution)/shard_map/scatter-add | solution.py:215
  841.1 10.2 broadcast_multiply_fusion
  851.3 13.2 reshape.344
  864.5 29.3 %scatter_custom_fusion.1 = f32[1025,1536]{1,0:T(8,128)} fusion(s32[2050]{0:T(1024)} %copy-done.52, f32[2050,1536]{1,0:T(8,128)} %reshape.344, f32[]{:T(128)} %constant.57.clone.1), kind=kCustom, calls=%fused_computation.91 | custom fusion | flops 3148800 | bytes 6298112 | tf_op jit(solution)/shard_map/scatter-add | solution.py:190
  898.8 10.8 reduce-scatter.10.cloned.1.call-done
  912.0 45.2 %reduce-scatter.8.cloned.1.call-done = bf16[256,1536]{1,0:T(8,128)(2,1)} async-done(((bf16[1024,1536]{1,0:T(8,128)(2,1)}), bf16[256,1536]{1,0:T(8,128)(2,1)}) %reduce-scatter.8.cloned.1.call-update) | async-done | bytes 786448 | tf_op jit(solution)/shard_map/reduce_scatter | solution.py:192
  970.2 11.1 all-to-all-done.4
  984.3 56.4 %while.29 = (s32[]{:T(128)}, f32[1024,2,64]{0,2,1:T(8,128)S(1)}, f32[1024,2,64]{0,2,1:T(8,128)}, bf16[2,512,2,3,64]{1,4,3,2,0:T(8,128)(2,1)}, bf16[2,512,2,3,64]...) while((s32[]{:T(128)}, f32[1024,2,64]{0,2,1:T(8,128)S(1)}, ...), condition=%wide.region_21.22_spmd.clone, body=%wide.region_19.21_spmd.clone.sunk | while | flops 2062022144 | bytes 184250800 | solution.py:270
  1002.9 6.6 fusion.164
  1045.2 6.8 fusion.77
  1060.7 9.5 all-to-all-done.5
  1079.0 7.9 fusion.74
  1086.9 6.8 fusion.67
  1093.9 27.6 %concatenate.55 = f32[1536,4098]{1,0:T(8,128)} concatenate(f32[1536,2560]{1,0:T(8,128)} %fusion.74, f32[1536,1536]{1,0:T(8,128)} %fusion.77, f32[1536,1]{1,0:T(8,128)S(1)} %stack.8, f32[1536,1]{1,0:T(8,128)S(1)} %copy-done.28), dimensions={1} | concatenate | bytes 50356224 | tf_op jit(solution)/shard_map/concatenate | solution.py:313
  1123.2 12.3 convert_bitcast_fusion.1
  1135.5 12.8 convert_bitcast_fusion.2
  1148.3 15.1 convert_bitcast_fusion
  1163.4 35.3 %pad_maximum_fusion = bf16[1536,10,1536]{0,2,1:T(8,128)(2,1)} fusion(bf16[1536,10,512]{0,2,1:T(8,128)(2,1)} %convert_bitcast_fusion, bf16[1536,10,512]{0,2,1:T(8,128)(2,1)} %convert_bitcast_fusion.1, bf16[1536,10,512]{0,2,1:T(8,128)(2,1)} %convert_bitcast_fusion.2), kind=kLoop, calls=%fused_computation.74 | loop fusion | flops 141557760 | bytes 94371840 | tf_op jit(solution)/shard_map/concatenate | solution.py:231
  1198.7 57.4 %copy.314 = bf16[1536,15360]{1,0:T(8,128)(2,1)} copy(bf16[1536,15360]{0,1:T(8,128)(2,1)} %bitcast.319) | data formatting | bytes 94371840
  1260.7 112.8 %reduce-scatter.12.cloned.1.call-done = f32[48,4098]{1,0:T(8,128)} async-done(((f32[1536,4098]{1,0:T(8,128)}), f32[48,4098]{1,0:T(8,128)}) %reduce-scatter.12.cloned.1.call-update) | async-done | bytes 786832 | tf_op jit(solution)/shard_map/reduce_scatter | solution.py:312
  1378.4 450.7 %reduce-scatter.16.cloned.1.call-done = bf16[192,15360]{1,0:T(8,128)(2,1)} async-done(((bf16[1536,15360]{1,0:T(8,128)(2,1)}), bf16[192,15360]{1,0:T(8,128)(2,1)}) %reduce-scatter.16.cloned.1.call-update) | async-done | bytes 5898256
  1829.2 9.7 copy.315
  1838.9 9.3 fusion.103
  (400 shorter events, 299.5 us)
Async XLA Ops:
  7.2 49.8 %copy-start.18 = (bf16[1,256,1536]{2,1,0:T(8,128)(2,1)S(1)}, bf16[1,256,1536]{2,1,0:T(8,128)(2,1)}, u32[]{:S(2)}) copy-start(bf16[1,256,1536]{2,1,0:T(8,128)(2,1)} %param.15) | copy-start | bytes 2359300
  7.2 82.1 %all-gather.10.cloned.1.call-start = ((), (), s32[]{:S(2)}) async-start(), calls=%async_computation.13 | async-start | bytes 8110080 | tf_op jit(solution)/shard_map/all_gather | solution.py:105
  7.9 172.3 %all-gather.12.cloned.1.call-start = ((), (), s32[]{:S(2)}) async-start(), calls=%async_computation.14 | async-start | bytes 4866048 | tf_op jit(solution)/shard_map/all_gather | solution.py:106
  52.3 42.5 %copy-start.29 = (f32[256,64]{0,1:T(8,128)}, f32[256,64]{0,1:T(8,128)S(1)}, u32[]{:S(2)}) copy-start(f32[256,64]{0,1:T(8,128)S(1)} %get-tuple-element.430) | copy-start | bytes 196612
  52.3 53.6 %copy-start.31 = (f32[256,64]{0,1:T(8,128)}, f32[256,64]{0,1:T(8,128)S(1)}, u32[]{:S(2)}) copy-start(f32[256,64]{0,1:T(8,128)S(1)} %get-tuple-element.431) | copy-start | bytes 196612
  57.0 37.8 %copy-start.39 = (f32[1536]{0:T(1024)}, f32[1536]{0:T(1024)S(1)}, u32[]{:S(2)}) copy-start(f32[1536]{0:T(1024)S(1)} %get-tuple-element.365) | copy-start | bytes 18436
  57.0 140.3 %copy-start.45 = (f32[1536]{0:T(1024)}, f32[1536]{0:T(1024)S(1)}, u32[]{:S(2)}) copy-start(f32[1536]{0:T(1024)S(1)} %get-tuple-element.364) | copy-start | bytes 18436
  57.2 37.6 %copy-start.58 = (f32[256]{0:T(256)}, f32[256]{0:T(256)S(1)}, u32[]{:S(2)}) copy-start(f32[256]{0:T(256)S(1)} %fusion.71) | copy-start | bytes 3076
  57.2 37.6 %copy-start.54 = (f32[256]{0:T(256)}, f32[256]{0:T(256)S(1)}, u32[]{:S(2)}) copy-start(f32[256]{0:T(256)S(1)} %fusion.97) | copy-start | bytes 3076
  108.1 9.4 all-to-all-start.1
  117.5 8.8 all-to-all-start.2
  126.2 17.9 all-to-all-start
  129.7 283.6 %all-gather.22.cloned.1.call-start = ((), (), s32[]{:S(2)}) async-start(), calls=%async_computation.23 | async-start | bytes 3932160 | tf_op jit(solution)/shard_map/all_gather | solution.py:196
  171.3 25.9 %copy-start.1 = (bf16[1024,2,64]{0,2,1:T(8,128)(2,1)}, bf16[1024,2,64]{0,2,1:T(8,128)(2,1)S(1)}, u32[]{:S(2)}) copy-start(bf16[1024,2,64]{0,2,1:T(8,128)(2,1)S(1)} %get-tuple-element.620) | copy-start | bytes 786436
  176.6 15.8 all-to-all-start.3
  180.1 323.1 %all-gather.14.cloned.1.call-start = ((), (), s32[]{:S(2)}) async-start(), calls=%async_computation.15 | async-start | bytes 3932160 | tf_op jit(solution)/shard_map/all_gather | solution.py:166
  197.2 94.6 %copy-start.60 = (f32[256]{0:T(256)}, f32[256]{0:T(256)S(1)}, u32[]{:S(2)}) copy-start(f32[256]{0:T(256)S(1)} %get-tuple-element.423) | copy-start | bytes 3076
  197.3 83.8 %copy-start.62 = (s32[1,1024]{1,0:T(1,128)S(1)}, s32[1,1024]{1,0:T(1,128)}, u32[]{:S(2)}) copy-start(s32[1,1024]{1,0:T(1,128)} %param.24) | copy-start | bytes 12292
  197.3 91.3 %copy-start.47 = (s32[1,1024,8]{1,2,0:T(8,128)S(1)}, s32[1,1024,8]{1,2,0:T(8,128)}, u32[]{:S(2)}) copy-start(s32[1,1024,8]{1,2,0:T(8,128)} %param.23) | copy-start | bytes 98308
  197.3 94.5 %copy-start.56 = (f32[256]{0:T(256)}, f32[256]{0:T(256)S(1)}, u32[]{:S(2)}) copy-start(f32[256]{0:T(256)S(1)} %fusion.98) | copy-start | bytes 3076
  199.5 336.6 %all-gather.16.cloned.1.call-start = ((), (), s32[]{:S(2)}) async-start(), calls=%async_computation.16 | async-start | bytes 17694720 | tf_op jit(solution)/shard_map/all_gather | solution.py:179
  200.1 423.8 %all-gather.18.cloned.1.call-start = ((), (), s32[]{:S(2)}) async-start(), calls=%async_computation.17 | async-start | bytes 17694720 | tf_op jit(solution)/shard_map/all_gather | solution.py:180
  200.6 565.6 %all-gather.20.cloned.1.call-start = ((), (), s32[]{:S(2)}) async-start(), calls=%async_computation.19 | async-start | bytes 17694720 | tf_op jit(solution)/shard_map/all_gather | solution.py:202
  201.4 708.2 %reduce-scatter.10.cloned.1.call-start = ((), (), s32[]{:S(2)}) async-start(), calls=%async_computation.20 | async-start | bytes 7864320 | tf_op jit(solution)/shard_map/reduce_scatter | solution.py:224
  201.4 25.9 %collective-permute-start = (bf16[192,10,512]{2,0,1:T(8,128)(2,1)S(1)}, bf16[192,10,512]{2,0,1:T(8,128)(2,1)S(1)}, u32[]{:S(2)}, u32[]{:S(2)}) collective-permute-start(bf16[192,10,512]{2,0,1:T(8,128)(2,1)S(1)} %copy-done.7), channel_id=1, source_target_pairs={{0,1},{1,2},{2,3},{3,4},{4,5},{5,6},{6,7},{7,0},{8,9},{9,10},{10,1... | collective-permute-start | bytes 5898248 | tf_op jit(solution)/shard_map/ppermute | solution.py:25
  227.4 53.7 %collective-permute-start.1 = (bf16[192,10,512]{2,0,1:T(8,128)(2,1)S(1)}, bf16[192,10,512]{2,0,1:T(8,128)(2,1)}, u32[]{:S(2)}, u32[]{:S(2)}) collective-permute-start(bf16[192,10,512]{2,0,1:T(8,128)(2,1)S(1)} %collective-permute-done), channel_id=1, source_target_pairs={{0,1},{1,2},{2,3},{3,4},{4,5},{5,6},{6,7},{7,0},{8,9},{9,10},{10,1... | collective-permute-start | bytes 5898248 | tf_op jit(solution)/shard_map/ppermute | solution.py:25
  227.4 57.2 %collective-permute-start.4 = (bf16[192,10,512]{2,0,1:T(8,128)(2,1)S(1)}, bf16[192,10,512]{2,0,1:T(8,128)(2,1)}, u32[]{:S(2)}, u32[]{:S(2)}) collective-permute-start(bf16[192,10,512]{2,0,1:T(8,128)(2,1)S(1)} %copy-done.7), channel_id=1, source_target_pairs={{0,7},{1,0},{2,1},{3,2},{4,3},{5,4},{6,5},{7,6},{8,15},{9,8},{10,9... | collective-permute-start | bytes 5898248 | tf_op jit(solution)/shard_map/ppermute | solution.py:27
  281.1 88.2 %collective-permute-start.2 = (bf16[192,10,512]{2,0,1:T(8,128)(2,1)}, bf16[192,10,512]{2,0,1:T(8,128)(2,1)}, u32[]{:S(2)}, u32[]{:S(2)}) collective-permute-start(bf16[192,10,512]{2,0,1:T(8,128)(2,1)} %collective-permute-done.1), channel_id=1, source_target_pairs={{0,1},{1,2},{2,3},{3,4},{4,5},{5,6},{6,7},{7,0},{8,9},{9,10},{10,1... | collective-permute-start | bytes 5898248 | tf_op jit(solution)/shard_map/ppermute | solution.py:25
  284.6 124.8 %collective-permute-start.5 = (bf16[192,10,512]{2,0,1:T(8,128)(2,1)}, bf16[192,10,512]{2,0,1:T(8,128)(2,1)}, u32[]{:S(2)}, u32[]{:S(2)}) collective-permute-start(bf16[192,10,512]{2,0,1:T(8,128)(2,1)} %collective-permute-done.4), channel_id=1, source_target_pairs={{0,7},{1,0},{2,1},{3,2},{4,3},{5,4},{6,5},{7,6},{8,15},{9,8},{10,9... | collective-permute-start | bytes 5898248 | tf_op jit(solution)/shard_map/ppermute | solution.py:27
  288.9 80.7 %copy-start.66 = (s32[2]{0:T(128)S(1)}, s32[2]{0:T(128)}, u32[]{:S(2)}) copy-start(s32[2]{0:T(128)} %constant.153) | copy-start | bytes 28
  289.0 80.9 %copy-start.65 = (s32[2]{0:T(128)S(1)}, s32[2]{0:T(128)}, u32[]{:S(2)}) copy-start(s32[2]{0:T(128)} %constant.156) | copy-start | bytes 28
  291.8 117.4 %copy-start.64 = (s32[2]{0:T(128)S(1)}, s32[2]{0:T(128)}, u32[]{:S(2)}) copy-start(s32[2]{0:T(128)} %constant.159) | copy-start | bytes 28
  291.8 117.5 %copy-start.63 = (s32[2]{0:T(128)S(1)}, s32[2]{0:T(128)}, u32[]{:S(2)}) copy-start(s32[2]{0:T(128)} %constant.162) | copy-start | bytes 28
  291.8 121.4 %copy-start.33 = (f32[1,1024,8]{1,2,0:T(8,128)S(1)}, f32[1,1024,8]{1,2,0:T(8,128)}, u32[]{:S(2)}) copy-start(f32[1,1024,8]{1,2,0:T(8,128)} %param.22) | copy-start | bytes 98308
  369.3 68.3 %collective-permute-start.3 = (bf16[192,10,512]{2,0,1:T(8,128)(2,1)}, bf16[192,10,512]{2,0,1:T(8,128)(2,1)}, u32[]{:S(2)}, u32[]{:S(2)}) collective-permute-start(bf16[192,10,512]{2,0,1:T(8,128)(2,1)} %collective-permute-done.2), channel_id=1, source_target_pairs={{0,1},{1,2},{2,3},{3,4},{4,5},{5,6},{6,7},{7,0},{8,9},{9,10},{10,1... | collective-permute-start | bytes 5898248 | tf_op jit(solution)/shard_map/ppermute | solution.py:25
  409.4 69.8 %collective-permute-start.6 = (bf16[192,10,512]{2,0,1:T(8,128)(2,1)}, bf16[192,10,512]{2,0,1:T(8,128)(2,1)}, u32[]{:S(2)}, u32[]{:S(2)}) collective-permute-start(bf16[192,10,512]{2,0,1:T(8,128)(2,1)} %collective-permute-done.5), channel_id=1, source_target_pairs={{0,7},{1,0},{2,1},{3,2},{4,3},{5,4},{6,5},{7,6},{8,15},{9,8},{10,9... | collective-permute-start | bytes 5898248 | tf_op jit(solution)/shard_map/ppermute | solution.py:27
  550.4 91.5 %copy-start.5 = (bf16[10,205,512]{2,1,0:T(8,128)(2,1)}, bf16[10,205,512]{2,1,0:T(8,128)(2,1)S(1)}, u32[]{:S(2)}) copy-start(bf16[10,205,512]{2,1,0:T(8,128)(2,1)S(1)} %get-tuple-element.425) | copy-start | bytes 6297604
  679.4 161.7 %copy-start.43 = (f32[10,205]{1,0:T(8,128)}, f32[10,205]{1,0:T(8,128)S(1)}, u32[]{:S(2)}) copy-start(f32[10,205]{1,0:T(8,128)S(1)} %reshape.321) | copy-start | bytes 24604
  695.6 81.7 %copy-start.11 = (bf16[10,205,512]{2,1,0:T(8,128)(2,1)}, bf16[10,205,512]{2,1,0:T(8,128)(2,1)S(1)}, u32[]{:S(2)}) copy-start(bf16[10,205,512]{2,1,0:T(8,128)(2,1)S(1)} %get-tuple-element.405) | copy-start | bytes 6297604
  841.0 116.1 %reduce-scatter.8.cloned.1.call-start = ((), (), s32[]{:S(2)}) async-start(), calls=%async_computation.18 | async-start | bytes 3932160 | tf_op jit(solution)/shard_map/reduce_scatter | solution.py:192
  893.8 63.4 %copy-start.23 = (bf16[1,256,1536]{2,1,0:T(8,128)(2,1)S(1)}, bf16[1,256,1536]{2,1,0:T(8,128)(2,1)}, u32[]{:S(2)}) copy-start(bf16[1,256,1536]{2,1,0:T(8,128)(2,1)} %param.25) | copy-start | bytes 2359300
  966.2 15.0 all-to-all-start.4
  1041.6 14.6 all-to-all-start.6
  1056.2 14.0 all-to-all-start.5
  1070.2 8.8 all-to-all-start.7
  1073.6 299.9 %reduce-scatter.12.cloned.1.call-start = ((), (), s32[]{:S(2)}) async-start(), calls=%async_computation.21 | async-start | bytes 26763264 | tf_op jit(solution)/shard_map/reduce_scatter | solution.py:312
  1121.6 707.6 %reduce-scatter.16.cloned.1.call-start = ((), (), s32[]{:S(2)}) async-start(), calls=%async_computation.24 | async-start | bytes 53084160
  1256.2 608.5 %reduce-scatter.14.cloned.1.call-start = ((), (), s32[]{:S(2)}) async-start(), calls=%async_computation.22 | async-start | bytes 40960 | tf_op jit(solution)/shard_map/reduce_scatter | solution.py:225
  (59 other events, 469.3 us)
Sparse Core Ops, SparseCore 0:
  11.0 78.1 all-gather.9
  92.3 64.6 all-gather.11
  158.9 46.3 all-gather.21
  207.5 43.6 all-gather.13
  252.7 226.2 all-gather.15
  480.5 143.3 all-gather.17
  625.5 140.6 all-gather.19
  841.2 68.4 reduce-scatter.9
  913.2 43.9 reduce-scatter.7
  1121.7 251.7 reduce-scatter.11
  1375.9 453.2 reduce-scatter.15
  1832.3 21.9 reduce-scatter.13
